TPU v7x, 256 devices: a whole 4x4x8 slice. The times are simulated.
256 devices in a mesh: dp: 2 (over core), tile: 32 (over x, z), chan: 4 (over y).
Axes of the slice: x: 4, y: 4, z: 8, core: 2. Of those that a mesh axis runs over, the one named last changes fastest.
Arguments:
- pixels: float32 [48, 65536], P(None, ('dp', 'tile')), may hold values from -6 to 6
- tile_slide: int32 [1024], P(('dp', 'tile')), may hold values from 0 to 63, as said below
- tile_count: int32 [64], P(('dp', 'tile')), may hold values from 8 to 16, as said below
- w_patch: float32 [96, 48], P('chan'), may hold values from -0.875 to 0.875
- b_patch: float32 [96], P('chan'), may hold values from -3 to 3
- dw_kernel: float32 [96, 49], P('chan'), may hold values from -0.875 to 0.875
- dw_bias: float32 [96], P('chan'), may hold values from -3 to 3
- layernorm_gain: float32 [96], P('chan'), may hold values from 0.25 to 1.75
- layernorm_bias: float32 [96], P('chan'), may hold values from -3 to 3
- w_up: float32 [384, 96], P('chan'), may hold values from -0.625 to 0.625
- b_up: float32 [384], P('chan'), may hold values from -3 to 3
- w_down: float32 [384, 96], P('chan'), may hold values from -0.3125 to 0.3125
- b_down: float32 [96], P('chan'), may hold values from -3 to 3
- w_head: float32 [96], P('chan'), may hold values from -3 to 3
- target: float32 [128], P(('dp', 'tile')), may hold values from -4 to 4
Outputs:
- g_w_patch: float32 [96, 48], P('chan')
- g_b_patch: float32 [96], P('chan')
- g_dw_kernel: float32 [96, 49], P('chan')
- g_dw_bias: float32 [96], P('chan')
- g_ln_gain: float32 [96], P('chan')
- g_ln_bias: float32 [96], P('chan')
- g_w_up: float32 [384, 96], P('chan')
- g_b_up: float32 [384], P('chan')
- g_w_down: float32 [384, 96], P('chan')
- g_b_down: float32 [96], P('chan')
- g_w_head: float32 [96], P('chan')
- loss: float32 [], replicated
Inputs may be any that keep to these rules, and one draw needn't show every extreme that they name: `tile_slide`: in every slide group a run of 4 consecutive slides, neither the group's first nor its last, receives no slot; other slides may receive none too. `tile_count`: at least 8 live slots a device; some device has all 16 live in every draw.
All inputs are finite; a program needn't handle non-finite values.
Results may differ from a plain program's by a relative error of at most 0.00029.
Values sent between devices are 32-bit elements; how exact they have to be, the bound alone decides.
A program may use at most 64 MiB of HBM per device.

v0:
```python
import jax
import jax.numpy as jnp
from jax import lax
from jax.sharding import PartitionSpec as P

SIDE = 8
epsilon = 1e-06
highest = lax.Precision.HIGHEST


def depthwise(stem_grid, kernel, bias):
    side_len = stem_grid.shape[-1]
    padded = jnp.pad(stem_grid, ((0, 0), (0, 0), (3, 3), (3, 3)))
    total = jnp.zeros_like(stem_grid)
    for kernel_row in range(7):
        for kernel_col in range(7):
            weight_tap = kernel[:, kernel_row * 7 + kernel_col][:, None, None, None]
            total = (
                total
                + weight_tap
                * padded[
                    :, :, kernel_row : kernel_row + side_len, kernel_col : kernel_col + side_len
                ]
            )
    return total + bias[:, None, None, None]


def stem_local(w_patch, b_patch, dw_kernel, dw_bias, pixels):
    local_width = w_patch.shape[0]
    tile_num = pixels.shape[1] // (SIDE * SIDE)
    stem = jnp.dot(w_patch, pixels, precision=highest) + b_patch[:, None]
    mixed_features = depthwise(
        stem.reshape(local_width, tile_num, SIDE, SIDE), dw_kernel, dw_bias
    ).reshape(local_width, -1)
    return (stem, mixed_features)


def channel_pool(stem, layer_out, b_down, onehot, tile_num):
    local_width = stem.shape[0]
    features = stem + layer_out + b_down[:, None]
    pooled = jnp.mean(features.reshape(local_width, tile_num, SIDE * SIDE), axis=2)
    return jnp.dot(onehot.T, pooled.T, precision=highest)


def features_grad(onehot, d_sums_all, local_width, tile_num):
    area = SIDE * SIDE
    d_pooled = jnp.dot(onehot, d_sums_all, precision=highest).T
    return jnp.broadcast_to((d_pooled / area)[:, :, None], (local_width, tile_num, area)).reshape(
        local_width, tile_num * area
    )


def per_device(
    pixels,
    tile_slide,
    tile_count,
    w_patch,
    b_patch,
    dw_kernel,
    dw_bias,
    layernorm_gain,
    layernorm_bias,
    w_up,
    b_up,
    w_down,
    b_down,
    w_head,
    target,
):
    chan_count = lax.axis_size("chan")
    local_width = w_patch.shape[0]
    channel_width = local_width * chan_count
    tile_num = tile_slide.shape[0]
    slide_dev = target.shape[0]
    group_slides = slide_dev * lax.axis_size("tile")
    all_slides = group_slides * lax.axis_size("dp")
    live = (jnp.arange(tile_num, dtype=jnp.int32) < tile_count[0]).astype(jnp.float32)
    onehot = (tile_slide[:, None] == jnp.arange(group_slides, dtype=jnp.int32)[None, :]).astype(
        jnp.float32
    ) * live[:, None]
    slide_count = jnp.sum(onehot, axis=0)
    (stem, mixed_features), stem_pull = jax.vjp(
        lambda a, b, c, d: stem_local(a, b, c, d, pixels), w_patch, b_patch, dw_kernel, dw_bias
    )
    totals = lax.psum(
        (jnp.sum(mixed_features, axis=0), jnp.sum(mixed_features * mixed_features, axis=0)), "chan"
    )
    average_value = totals[0] / channel_width
    variance = totals[1] / channel_width - average_value * average_value
    inverse_deviation = lax.rsqrt(variance + epsilon)
    centered_input = (mixed_features - average_value) * inverse_deviation
    normalized_rows = centered_input * layernorm_gain[:, None] + layernorm_bias[:, None]
    normed_all = lax.all_gather(normalized_rows, "chan", axis=0, tiled=True)
    pre_act = jnp.dot(w_up, normed_all, precision=highest) + b_up[:, None]
    hidden, gelu_pull = jax.vjp(lambda value: jax.nn.gelu(value, approximate=False), pre_act)
    columns = w_down
    layer_out = lax.psum_scatter(
        jnp.dot(columns.T, hidden, precision=highest), "chan", scatter_dimension=0, tiled=True
    )
    slide_part = channel_pool(stem, layer_out, b_down, onehot, tile_num)
    owned_sums, owned_counts = (
        lax.psum_scatter(slide_part, "tile", scatter_dimension=0, tiled=True),
        lax.psum_scatter(slide_count, "tile", scatter_dimension=0, tiled=True),
    )
    counts = jnp.maximum(owned_counts, 1.0)
    slide_feat = owned_sums / counts[:, None]
    logit = lax.psum(jnp.dot(slide_feat, w_head, precision=highest), "chan")
    error = logit - target
    loss_part = 0.5 * jnp.sum(error * error) / all_slides
    d_logit = error / all_slides
    g_head = jnp.dot(slide_feat.T, d_logit, precision=highest)
    d_sums = d_logit[:, None] * w_head[None, :] / counts[:, None]
    d_sums_all = lax.all_gather(d_sums, "tile", axis=0, tiled=True)
    d_features = features_grad(onehot, d_sums_all, local_width, tile_num)
    g_b_down = jnp.sum(d_features, axis=1)
    d_out_all = lax.all_gather(d_features, "chan", axis=0, tiled=True)
    g_w_down = jnp.dot(hidden, d_out_all.T, precision=highest)
    d_hidden = jnp.dot(w_down, d_out_all, precision=highest)
    d_pre = gelu_pull(d_hidden)[0]
    g_w_up = jnp.dot(d_pre, normed_all.T, precision=highest)
    g_b_up = jnp.sum(d_pre, axis=1)
    columns = w_up
    normalized_gradient = lax.psum_scatter(
        jnp.dot(columns.T, d_pre, precision=highest), "chan", scatter_dimension=0, tiled=True
    )
    gain_gradient = jnp.sum(normalized_gradient * centered_input, axis=1)
    g_shift = jnp.sum(normalized_gradient, axis=1)
    centered_gradient = normalized_gradient * layernorm_gain[:, None]
    backward_sums = lax.psum(
        (jnp.sum(centered_gradient, axis=0), jnp.sum(centered_gradient * centered_input, axis=0)),
        "chan",
    )
    mixed_gradient = inverse_deviation * (
        centered_gradient
        - backward_sums[0] / channel_width
        - centered_input * (backward_sums[1] / channel_width)
    )
    g_patch, g_bpatch, g_kernel, g_dwbias = stem_pull((d_features, mixed_gradient))
    summed = lax.psum(
        (
            g_patch,
            g_bpatch,
            g_kernel,
            g_dwbias,
            gain_gradient,
            g_shift,
            g_w_up,
            g_b_up,
            g_w_down,
            g_b_down,
            g_head,
            loss_part,
        ),
        ("dp", "tile"),
    )
    return summed


def solution(mesh):
    in_specs = (
        P(None, ("dp", "tile")),
        P(("dp", "tile")),
        P(("dp", "tile")),
        P("chan", None),
        P("chan"),
        P("chan", None),
        P("chan"),
        P("chan"),
        P("chan"),
        P("chan", None),
        P("chan"),
        P("chan", None),
        P("chan"),
        P("chan"),
        P(("dp", "tile")),
    )
    out_specs = (
        P("chan", None),
        P("chan"),
        P("chan", None),
        P("chan"),
        P("chan"),
        P("chan"),
        P("chan", None),
        P("chan"),
        P("chan", None),
        P("chan"),
        P("chan"),
        P(),
    )
    return jax.shard_map(
        per_device, mesh=mesh, in_specs=in_specs, out_specs=out_specs, check_vma=False
    )
```

profile of v0, /device:TPU:1, one launch (start us, length us, event | category | flops | bytes accessed | tf_op | source)
XLA Modules:
  0.0 583.6 jit_solution(18157848405234515097)
XLA Ops:
  7.3 1.5 slice_reduce_fusion.46
  8.8 2.0 slice_reduce_fusion.48
  10.7 2.0 slice_reduce_fusion.47
  12.7 1.0 convolution_add_fusion.1
  13.9 4.0 fusion.39
  18.3 9.6 %all-reduce.104 = (f32[1024]{0:T(1024)S(1)}, f32[1024]{0:T(1024)S(1)}) all-reduce(f32[1024]{0:T(1024)S(1)} %reduce_sum.554, f32[1024]{0:T(1024)S(1)} %reduce_sum.552), channel_id=1, replica_groups=mesh['dp'=2,'tile'=32,'chan'=4] {'chan'}, use_global_device_ids=true, to_apply=%region_3.4 | all-reduce | flops 2048 | bytes 16384 | tf_op jit(solution)/shard_map/psum | solution.py:85
  28.0 10.9 %all_gather.9 = f32[96,1024]{1,0:T(8,128)S(1)} all-gather(f32[24,1024]{1,0:T(8,128)S(1)} %multiply_add_fusion), channel_id=1, replica_groups=mesh['dp'=2,'tile'=32,'chan'=4] {'chan'}, dimensions={0}, use_global_device_ids=true | all-gather | bytes 491520 | tf_op jit(solution)/shard_map/all_gather | solution.py:93
  38.9 1.3 fusion
  40.3 1.3 convolution_bitcast_fusion.2
  43.6 24.4 %reduce-scatter.3.cloned.1.call-done = f32[24,1024]{1,0:T(8,128)} async-done(((f32[96,1024]{1,0:T(8,128)}), f32[24,1024]{1,0:T(8,128)}) %reduce-scatter.3.cloned.1.call-update) | async-done | bytes 98320 | tf_op jit(solution)/shard_map/reduce_scatter | solution.py:97
  68.0 1.0 add_add_fusion.1
  69.6 115.5 %all-reduce.102 = (f32[64]{0:T(128)S(1)}, f32[64,24]{1,0:T(8,128)S(1)}) all-reduce(f32[64]{0:T(128)S(1)} %select_reduce_fusion, f32[64,24]{1,0:T(8,128)S(1)} %fusion.21), channel_id=4, replica_groups=mesh['dp'=2,'tile'=32,'chan'=4] {'tile'}, use_global_device_ids=true, to_apply=%region_8.9.clone | all-reduce | flops 1600 | bytes 12800
  185.4 7.3 %psum.121 = f32[2]{0:T(128)S(1)} all-reduce(f32[2]{0:T(128)S(1)} %convolution_bitcast_fusion.4), channel_id=1, replica_groups=mesh['dp'=2,'tile'=32,'chan'=4] {'chan'}, use_global_device_ids=true, to_apply=%region_9.10 | all-reduce | flops 2 | bytes 16 | tf_op jit(solution)/shard_map/psum | solution.py:107
  192.6 0.6 multiply_reduce_fusion.53
  193.3 30.8 %all-gather = f32[32,2,24]{2,1,0:T(2,128)S(1)} all-gather(f32[1,2,24]{2,1,0:T(2,128)S(1)} %divide_bitcast_fusion), channel_id=1, replica_groups=mesh['dp'=2,'tile'=32,'chan'=4] {'tile'}, dimensions={0}, use_global_device_ids=true | all-gather | bytes 6336 | tf_op jit(solution)/shard_map/all_gather | solution.py:113
  224.6 9.9 %all_gather.11 = f32[96,1024]{1,0:T(8,128)S(1)} all-gather(f32[24,1024]{1,0:T(8,128)S(1)} %copy.43), channel_id=1, replica_groups=mesh['dp'=2,'tile'=32,'chan'=4] {'chan'}, dimensions={0}, use_global_device_ids=true | all-gather | bytes 491520 | tf_op jit(solution)/shard_map/all_gather | solution.py:116
  234.5 0.7 fusion.41
  235.2 1.3 convolution_bitcast_fusion
  238.4 57.9 %reduce-scatter.5.cloned.1.call-done = f32[24,1024]{1,0:T(8,128)} async-done(((f32[96,1024]{1,0:T(8,128)}), f32[24,1024]{1,0:T(8,128)}) %reduce-scatter.5.cloned.1.call-update) | async-done | bytes 98320 | tf_op jit(solution)/shard_map/reduce_scatter | solution.py:123
  296.3 1.1 multiply_reduce_fusion.49
  297.4 7.4 %all-reduce.103 = (f32[1024]{0:T(1024)S(1)}, f32[1024]{0:T(1024)S(1)}) all-reduce(f32[1024]{0:T(1024)S(1)} %get-tuple-element.111, f32[1024]{0:T(1024)S(1)} %get-tuple-element.112), channel_id=1, replica_groups=mesh['dp'=2,'tile'=32,'chan'=4] {'chan'}, use_global_device_ids=true, to_apply=%region_14.15 | all-reduce | flops 2048 | bytes 16384 | tf_op jit(solution)/shard_map/psum | solution.py:129
  304.9 1.1 fusion.40
  306.2 0.8 multiply_reduce_fusion.45
  307.0 1.5 multiply_reduce_fusion.46
  308.5 1.3 multiply_reduce_fusion.47
  309.9 0.9 broadcast_multiply_fusion.2
  310.7 1.2 broadcast_multiply_fusion.1
  312.0 1.2 broadcast_multiply_fusion
  313.2 5.1 pad_add_fusion
  318.7 1.0 fusion.42
  319.8 256.4 %all-reduce.106 = (f32[24,48]{1,0:T(8,128)}, f32[24]{0:T(128)}, f32[24,49]{0,1:T(8,128)S(1)}, f32[24]{0:T(128)}, f32[24]{0:T(128)}, /*index=5*/f32[24]{0:T(128)}...) all-reduce(f32[24,48]{1,0:T(8,128)S(1)} %fusion.42, ...), channel_id=1, replica_groups=mesh['dp'=2,'tile'=32,'chan'=4] {'dp','tile'}, use_global_device_ids=true, to_apply=%region_15.16 | all-reduce | flops 21001 | bytes 168008 | tf_op jit(solution)/shard_map/psum | solution.py:139
  576.1 0.7 copy.45
  (55 shorter events, 4.8 us)
Async XLA Ops:
  7.2 5.5 copy-start
  7.2 20.7 %copy-start.3 = (f32[24]{0:T(128)S(1)}, f32[24]{0:T(128)}, u32[]{:S(2)}) copy-start(f32[24]{0:T(128)} %param.22) | copy-start | bytes 292
  7.2 20.7 %copy-start.4 = (f32[24]{0:T(128)S(1)}, f32[24]{0:T(128)}, u32[]{:S(2)}) copy-start(f32[24]{0:T(128)} %param.23) | copy-start | bytes 292
  7.2 60.8 %reduce-scatter.3.cloned.1.call-start = ((), (), s32[]{:S(2)}) async-start(), calls=%async_computation.2 | async-start | bytes 491520 | tf_op jit(solution)/shard_map/reduce_scatter | solution.py:97
  12.7 26.2 %copy-start.2 = (f32[96,96]{1,0:T(8,128)S(1)}, f32[96,96]{1,0:T(8,128)}, u32[]{:S(2)}) copy-start(f32[96,96]{1,0:T(8,128)} %param.24) | copy-start | bytes 110596
  12.7 26.2 %copy-start.8 = (f32[96]{0:T(128)S(1)}, f32[96]{0:T(128)}, u32[]{:S(2)}) copy-start(f32[96]{0:T(128)} %param.25) | copy-start | bytes 1156
  38.9 1.4 copy-start.1
  38.9 3.4 copy-start.10
  38.9 4.6 copy-start.9
  38.9 29.1 %copy-start.5 = (f32[24]{0:T(128)S(1)}, f32[24]{0:T(128)}, u32[]{:S(2)}) copy-start(f32[24]{0:T(128)} %param.27) | copy-start | bytes 292
  40.2 145.0 %copy-start.6 = (f32[24]{0:T(128)S(1)}, f32[24]{0:T(128)}, u32[]{:S(2)}) copy-start(f32[24]{0:T(128)} %param.28) | copy-start | bytes 292
  40.2 152.4 %copy-start.7 = (f32[2]{0:T(128)S(1)}, f32[2]{0:T(128)}, u32[]{:S(2)}) copy-start(f32[2]{0:T(128)} %param.29) | copy-start | bytes 28
  41.6 254.8 %reduce-scatter.5.cloned.1.call-start = ((), (), s32[]{:S(2)}) async-start(), calls=%async_computation.3 | async-start | bytes 491520 | tf_op jit(solution)/shard_map/reduce_scatter | solution.py:123
Sparse Core Ops, SparseCore 0:
  41.7 26.2 reduce-scatter.2
  236.6 59.6 reduce-scatter.4
where the time goes:
time: 584 us
  blocking collectives  448 us (77%)
  waiting for transfers between devices  82.3 us (14%)
  other arithmetic  21 us (4%)
  between operations  16.3 us (3%)
  matrix products  8.16 us (1%)
  local copies, waits for them, and re-layouts  7.87 us (1%)
    psum x1, blocking collectives, per_device(): lax.psum((g_patch, g_bpatch, g_kernel, g_dwbias, gain_gradient, g_shift,...  256 us
    unnamed x1, blocking collectives  116 us
    reduce_scatter x1, waiting for transfers between devices, per_device(): lax.psum_scatter(jnp.dot(columns.T, d_pre, precision=highest), 'chan', sc...  57.9 us
    all_gather x1, blocking collectives, per_device(): d_sums_all = lax.all_gather(d_sums, 'tile', axis=0, tiled=True)  30.8 us
    reduce_scatter x1, waiting for transfers between devices, per_device(): lax.psum_scatter(jnp.dot(columns.T, hidden, precision=highest), 'chan', s...  24.4 us
  transfers between devices with their start and end apart: 2, of which 2 were waited for; matrix products, arithmetic and copies ran while one was open for 0% of the time, Pallas kernels for 0%

commit v1 on v0

--- a/solution.py
+++ b/solution.py
@@ -110,7 +110,9 @@
     d_logit = error / all_slides
     g_head = jnp.dot(slide_feat.T, d_logit, precision=highest)
     d_sums = d_logit[:, None] * w_head[None, :] / counts[:, None]
-    d_sums_all = lax.all_gather(d_sums, "tile", axis=0, tiled=True)
+    d_sums_all = jnp.concatenate(
+        lax.all_to_all(jnp.stack([d_sums] * lax.axis_size("tile")), "tile", 0, 0), axis=0
+    )
     d_features = features_grad(onehot, d_sums_all, local_width, tile_num)
     g_b_down = jnp.sum(d_features, axis=1)
     d_out_all = lax.all_gather(d_features, "chan", axis=0, tiled=True)

time: 584 us -> 555 us (0.950)
  blocking collectives: 448 us -> 429 us
  waiting for transfers between devices: 82.3 us -> 72 us
    all_gather x1 -> x0, blocking collectives: 30.8 us -> none  [per_device(): d_sums_all = lax.all_gather(d_sums, 'tile', axis=0, tiled=True)]
    all_to_all x0 -> x1, blocking collectives: none -> 11.7 us  [per_device(): lax.all_to_all(jnp.stack([d_sums] * lax.axis_size('tile')), 'tile', 0, 0)]
    reduce_scatter x1, waiting for transfers between devices: 57.9 us -> 47.6 us  [per_device(): lax.psum_scatter(jnp.dot(columns.T, d_pre, precision=highest), 'chan', sc...]
where the time goes in v1:
time: 555 us; the launch traced here: 554 us
  blocking collectives  429 us (77%)
  waiting for transfers between devices  72 us (13%)
  other arithmetic  21 us (4%)
  between operations  16.3 us (3%)
  matrix products  8.16 us (1%)
  local copies, waits for them, and re-layouts  7.88 us (1%)
    psum x1, blocking collectives, per_device(): lax.psum((g_patch, g_bpatch, g_kernel, g_dwbias, gain_gradient, g_shift,...  256 us
    unnamed x1, blocking collectives  116 us
    reduce_scatter x1, waiting for transfers between devices, per_device(): lax.psum_scatter(jnp.dot(columns.T, d_pre, precision=highest), 'chan', sc...  47.6 us
    reduce_scatter x1, waiting for transfers between devices, per_device(): lax.psum_scatter(jnp.dot(columns.T, hidden, precision=highest), 'chan', s...  24.4 us
    all_to_all x1, blocking collectives, per_device(): lax.all_to_all(jnp.stack([d_sums] * lax.axis_size('tile')), 'tile', 0, 0)  11.7 us
  transfers between devices with their start and end apart: 2, of which 2 were waited for; matrix products, arithmetic and copies ran while one was open for 0% of the time, Pallas kernels for 0%

profile of v1, /device:TPU:1, one launch (start us, length us, event | category | flops | bytes accessed | tf_op | source)
XLA Modules:
  0.0 554.1 jit_solution(8955730366489301886)
XLA Ops:
  7.3 1.5 slice_reduce_fusion.46
  8.8 2.0 slice_reduce_fusion.48
  10.7 2.0 slice_reduce_fusion.47
  12.7 1.0 convolution_add_fusion.1
  13.9 4.0 fusion.39
  18.3 9.6 %all-reduce.104 = (f32[1024]{0:T(1024)S(1)}, f32[1024]{0:T(1024)S(1)}) all-reduce(f32[1024]{0:T(1024)S(1)} %reduce_sum.554, f32[1024]{0:T(1024)S(1)} %reduce_sum.552), channel_id=1, replica_groups=mesh['dp'=2,'tile'=32,'chan'=4] {'chan'}, use_global_device_ids=true, to_apply=%region_3.4 | all-reduce | flops 2048 | bytes 16384 | tf_op jit(solution)/shard_map/psum | solution.py:85
  28.0 10.9 %all_gather.6 = f32[96,1024]{1,0:T(8,128)S(1)} all-gather(f32[24,1024]{1,0:T(8,128)S(1)} %multiply_add_fusion), channel_id=1, replica_groups=mesh['dp'=2,'tile'=32,'chan'=4] {'chan'}, dimensions={0}, use_global_device_ids=true | all-gather | bytes 491520 | tf_op jit(solution)/shard_map/all_gather | solution.py:93
  38.9 1.3 fusion
  40.3 1.3 convolution_bitcast_fusion.2
  43.6 24.4 %reduce-scatter.3.cloned.1.call-done = f32[24,1024]{1,0:T(8,128)} async-done(((f32[96,1024]{1,0:T(8,128)}), f32[24,1024]{1,0:T(8,128)}) %reduce-scatter.3.cloned.1.call-update) | async-done | bytes 98320 | tf_op jit(solution)/shard_map/reduce_scatter | solution.py:97
  68.0 1.0 add_add_fusion.1
  69.6 115.5 %all-reduce.102 = (f32[64]{0:T(128)S(1)}, f32[64,24]{1,0:T(8,128)S(1)}) all-reduce(f32[64]{0:T(128)S(1)} %select_reduce_fusion, f32[64,24]{1,0:T(8,128)S(1)} %fusion.21), channel_id=4, replica_groups=mesh['dp'=2,'tile'=32,'chan'=4] {'tile'}, use_global_device_ids=true, to_apply=%region_8.9.clone | all-reduce | flops 1600 | bytes 12800
  185.4 7.3 %psum.121 = f32[2]{0:T(128)S(1)} all-reduce(f32[2]{0:T(128)S(1)} %convolution_bitcast_fusion.4), channel_id=1, replica_groups=mesh['dp'=2,'tile'=32,'chan'=4] {'chan'}, use_global_device_ids=true, to_apply=%region_9.10 | all-reduce | flops 2 | bytes 16 | tf_op jit(solution)/shard_map/psum | solution.py:107
  192.6 0.6 multiply_reduce_fusion.53
  193.3 11.7 %all_to_all.5 = f32[32,2,24]{2,1,0:T(2,128)S(1)} all-to-all(f32[32,2,24]{2,1,0:T(2,128)S(1)} %stack.2), channel_id=1, replica_groups=mesh['dp'=2,'tile'=32,'chan'=4] {'tile'}, dimensions={0} | all-to-all | bytes 12288 | tf_op jit(solution)/shard_map/all_to_all | solution.py:114
  205.4 9.9 %all_gather.7 = f32[96,1024]{1,0:T(8,128)S(1)} all-gather(f32[24,1024]{1,0:T(8,128)S(1)} %copy.43), channel_id=1, replica_groups=mesh['dp'=2,'tile'=32,'chan'=4] {'chan'}, dimensions={0}, use_global_device_ids=true | all-gather | bytes 491520 | tf_op jit(solution)/shard_map/all_gather | solution.py:118
  215.3 0.7 fusion.41
  216.0 1.3 convolution_bitcast_fusion
  219.2 47.6 %reduce-scatter.5.cloned.1.call-done = f32[24,1024]{1,0:T(8,128)} async-done(((f32[96,1024]{1,0:T(8,128)}), f32[24,1024]{1,0:T(8,128)}) %reduce-scatter.5.cloned.1.call-update) | async-done | bytes 98320 | tf_op jit(solution)/shard_map/reduce_scatter | solution.py:125
  266.8 1.1 multiply_reduce_fusion.49
  267.9 7.4 %all-reduce.103 = (f32[1024]{0:T(1024)S(1)}, f32[1024]{0:T(1024)S(1)}) all-reduce(f32[1024]{0:T(1024)S(1)} %get-tuple-element.111, f32[1024]{0:T(1024)S(1)} %get-tuple-element.112), channel_id=1, replica_groups=mesh['dp'=2,'tile'=32,'chan'=4] {'chan'}, use_global_device_ids=true, to_apply=%region_14.15 | all-reduce | flops 2048 | bytes 16384 | tf_op jit(solution)/shard_map/psum | solution.py:131
  275.4 1.1 fusion.40
  276.7 0.8 multiply_reduce_fusion.45
  277.5 1.5 multiply_reduce_fusion.46
  279.0 1.3 multiply_reduce_fusion.47
  280.4 0.9 broadcast_multiply_fusion.2
  281.2 1.2 broadcast_multiply_fusion.1
  282.5 1.2 broadcast_multiply_fusion
  283.7 5.1 pad_add_fusion
  289.2 1.0 fusion.42
  290.3 256.3 %all-reduce.106 = (f32[24,48]{1,0:T(8,128)}, f32[24]{0:T(128)}, f32[24,49]{0,1:T(8,128)S(1)}, f32[24]{0:T(128)}, f32[24]{0:T(128)}, /*index=5*/f32[24]{0:T(128)}...) all-reduce(f32[24,48]{1,0:T(8,128)S(1)} %fusion.42, ...), channel_id=1, replica_groups=mesh['dp'=2,'tile'=32,'chan'=4] {'dp','tile'}, use_global_device_ids=true, to_apply=%region_15.16 | all-reduce | flops 21001 | bytes 168008 | tf_op jit(solution)/shard_map/psum | solution.py:141
  546.6 0.7 copy.45
  (56 shorter events, 4.8 us)
Async XLA Ops:
  7.2 5.5 copy-start
  7.2 20.7 %copy-start.3 = (f32[24]{0:T(128)S(1)}, f32[24]{0:T(128)}, u32[]{:S(2)}) copy-start(f32[24]{0:T(128)} %param.22) | copy-start | bytes 292
  7.2 20.7 %copy-start.4 = (f32[24]{0:T(128)S(1)}, f32[24]{0:T(128)}, u32[]{:S(2)}) copy-start(f32[24]{0:T(128)} %param.23) | copy-start | bytes 292
  7.2 60.8 %reduce-scatter.3.cloned.1.call-start = ((), (), s32[]{:S(2)}) async-start(), calls=%async_computation.3 | async-start | bytes 491520 | tf_op jit(solution)/shard_map/reduce_scatter | solution.py:97
  12.7 26.2 %copy-start.2 = (f32[96,96]{1,0:T(8,128)S(1)}, f32[96,96]{1,0:T(8,128)}, u32[]{:S(2)}) copy-start(f32[96,96]{1,0:T(8,128)} %param.24) | copy-start | bytes 110596
  12.7 26.2 %copy-start.8 = (f32[96]{0:T(128)S(1)}, f32[96]{0:T(128)}, u32[]{:S(2)}) copy-start(f32[96]{0:T(128)} %param.25) | copy-start | bytes 1156
  38.9 1.4 copy-start.1
  38.9 3.4 copy-start.10
  38.9 4.6 copy-start.9
  38.9 29.1 %copy-start.5 = (f32[24]{0:T(128)S(1)}, f32[24]{0:T(128)}, u32[]{:S(2)}) copy-start(f32[24]{0:T(128)} %param.27) | copy-start | bytes 292
  40.2 145.0 %copy-start.6 = (f32[24]{0:T(128)S(1)}, f32[24]{0:T(128)}, u32[]{:S(2)}) copy-start(f32[24]{0:T(128)} %param.28) | copy-start | bytes 292
  40.2 152.4 %copy-start.7 = (f32[2]{0:T(128)S(1)}, f32[2]{0:T(128)}, u32[]{:S(2)}) copy-start(f32[2]{0:T(128)} %param.29) | copy-start | bytes 28
  41.6 225.3 %reduce-scatter.5.cloned.1.call-start = ((), (), s32[]{:S(2)}) async-start(), calls=%async_computation.4 | async-start | bytes 491520 | tf_op jit(solution)/shard_map/reduce_scatter | solution.py:125
Sparse Core Ops, SparseCore 0:
  41.7 26.2 reduce-scatter.2
  217.5 49.3 reduce-scatter.4
